TPU v7x, 512 devices: a whole 4x4x16 slice. The times are simulated.
512 devices in a mesh: line: 8 (over y_hi, x), bus: 32 (over y_lo, z), scen: 2 (over core).
Axes of the slice: x: 4, y: 4 (y_hi: 2, y_lo: 2; y = y_hi * 2 + y_lo), z: 16, core: 2. Of those that a mesh axis runs over, the one named last changes fastest.
Arguments:
- ptdf: bfloat16 [8192, 49152], P('line', 'bus'), may hold values from -0.0546875 to 0.0546875
- injections: bfloat16 [49152, 512], P('bus', 'scen'), may hold values from -6 to 6
- lodf: bfloat16 [8192, 2048], P(('line', 'bus')), may hold values from -3 to 3
- ratings: float32 [8192], P(('line', 'bus')), may hold values from 0.5 to 2
- outages: int32 [2048], replicated, may hold values from 0 to 8191, as said below
Outputs:
- overload: float32 [8192, 2048], P(('line', 'bus'))
Inputs may be any that keep to these rules, and one draw needn't show every extreme that they name: `outages`: 2048 distinct line indices.
All inputs are finite; a program needn't handle non-finite values.
Results may differ from a plain program's by a relative error of at most 0.0003.
Values sent between devices are 32-bit elements; how exact they have to be, the bound alone decides.
No kernel may reach another device: no remote copies, remote signals or barrier semaphores. Data moves between devices by JAX's collectives and lax.ppermute only.
A program may use at most 64 MiB of HBM per device.

v0:
```python
import jax
import jax.numpy as jnp
from jax import lax
from jax.sharding import PartitionSpec as P

softness = 0.2


def base_flow_term(base_rows, lodf_rows, outage_flow):
    return (
        base_rows[:, None, :] + lodf_rows.astype(jnp.float32)[:, :, None] * outage_flow[None, :, :]
    )


def overload_sum(base_flow, outage_flow, lodf, ratings):
    lines_here = base_flow.shape[0]
    groups = lines_here // 4

    def line_block(pieces):
        base_rows, lodf_rows, rating_rows = pieces
        post_flow = base_flow_term(base_rows, lodf_rows, outage_flow)
        margin = (jnp.abs(post_flow) - rating_rows[:, None, None]) / (
            softness * rating_rows[:, None, None]
        )
        return jnp.sum(jax.nn.sigmoid(margin), axis=2)

    summed = lax.map(
        line_block,
        (base_flow.reshape(groups, 4, -1), lodf.reshape(groups, 4, -1), ratings.reshape(groups, 4)),
    )
    return summed.reshape(lines_here, -1)


def select_rows(flows, outages, first):
    count = flows.shape[0]
    offset = outages - first
    inside = (offset >= 0) & (offset < count)
    picked = jnp.take(flows, jnp.clip(offset, 0, count - 1), axis=0)
    return jnp.where(inside[:, None], picked, 0.0)


def shards(ptdf, injections, lodf, ratings, outages):
    own_rows = lodf.shape[0]
    base_flow = lax.psum_scatter(
        jnp.dot(ptdf, injections, preferred_element_type=jnp.float32),
        "bus",
        scatter_dimension=0,
        tiled=True,
    )
    first_own = (lax.axis_index("line") * lax.axis_size("bus") + lax.axis_index("bus")) * own_rows
    outage_flow = lax.psum(select_rows(base_flow, outages, first_own), ("line", "bus"))
    local_sum = overload_sum(base_flow, outage_flow, lodf, ratings)
    total = lax.psum(local_sum, "scen")
    return total / (injections.shape[1] * lax.axis_size("scen"))


def solution(mesh):
    return jax.shard_map(
        shards,
        mesh=mesh,
        in_specs=(
            P("line", "bus"),
            P("bus", "scen"),
            P(("line", "bus"), None),
            P(("line", "bus")),
            P(),
        ),
        out_specs=P(("line", "bus"), None),
        check_vma=False,
    )
```

profile of v0, /device:TPU:1, one launch (start us, length us, event | category | flops | bytes accessed | tf_op | source)
XLA Modules:
  0.0 666.5 jit_solution(12721925452298086936)
XLA Ops:
  6.5 0.0 copy-start
  6.5 0.0 copy-start.3
  6.5 0.0 reduce-scatter.2.cloned.1.call-start
  6.5 1.9 copy-done
  8.4 3.1 fusion.4
  11.5 0.0 reduce-scatter.2.cloned.1.call-update
  11.5 0.0 all-reduce.3.cloned.1.call-start
  11.6 0.0 copy-done.3
  11.6 118.5 %reduce-scatter.2.cloned.1.call-done = f32[32,256]{1,0:T(8,128)} async-done(((f32[1024,256]{1,0:T(8,128)}), f32[32,256]{1,0:T(8,128)}) %reduce-scatter.2.cloned.1.call-update) | async-done | bytes 32784 | tf_op jit(solution)/shard_map/reduce_scatter | solution.py:44
  130.1 9.3 %gather_fusion = f32[2048,256]{1,0:T(8,128)} fusion(f32[32,256]{1,0:T(8,128)} %reduce-scatter.2.cloned.1.call-done, s32[2048]{0:T(1024)S(1)} %fusion.2), kind=kCustom, calls=%fused_computation | custom fusion | bytes 4202496 | tf_op jit(solution)/shard_map/jit(_take)/gather | solution.py:38
  139.4 0.0 copy-start.2
  139.4 0.0 copy-start.4
  139.4 0.0 copy-start.1
  139.4 4.3 select_select_fusion
  143.8 0.0 all-reduce.3.cloned.1.call-update
  143.8 0.0 all-reduce.5.cloned.1.call-start
  143.9 0.0 copy-done.2
  143.9 0.1 reshape.38
  143.9 0.0 copy-done.4
  143.9 0.1 reshape.39
  144.0 0.0 copy-done.1
  144.0 420.5 %all-reduce.3.cloned.1.call-done = f32[2048,256]{1,0:T(8,128)} async-done(((f32[2048,256]{1,0:T(8,128)}), f32[2048,256]{1,0:T(8,128)}) %all-reduce.3.cloned.1.call-update) | async-done | bytes 2097168 | tf_op jit(solution)/shard_map/psum | solution.py:51
  564.5 46.5 %while.10 = (s32[]{:T(128)}, f32[8,4,2048]{2,1,0:T(4,128)}, f32[8,4,256]{2,1,0:T(4,128)S(1)}, bf16[8,4,2048]{2,1,0:T(4,128)(2,1)S(1)}, f32[2048,256]{1,0:T(8,128)}, /*index=5*/f32[8,4]{1,0:T(8,128)S(1)}, s32[]{:T(128)}) while((s32[]{:T(128)}, f32[8,4,2048]{2,1,0:T(4,128)}, f32[8,4,256]{2,1,0:T(4,128)S(1)}, bf16[8,4,2048]{2,1,0:T(4,128)(2,1)S(1)}, ...), condition=%wide.region_4.5_spmd, body=%wide.region_2.4_spmd.sunk | while | flops 18874372 | bytes 2290345 | solution.py:27
  564.5 5.1 fusion.8
  569.7 0.6 bitcast_dynamic-update-slice_fusion.2
  570.4 5.1 fusion.8
  575.5 0.6 bitcast_dynamic-update-slice_fusion.2
  576.2 5.1 fusion.8
  581.3 0.6 bitcast_dynamic-update-slice_fusion.2
  582.0 5.1 fusion.8
  587.1 0.6 bitcast_dynamic-update-slice_fusion.2
  587.8 5.1 fusion.8
  592.9 0.6 bitcast_dynamic-update-slice_fusion.2
  593.6 5.1 fusion.8
  598.7 0.6 bitcast_dynamic-update-slice_fusion.2
  599.4 5.1 fusion.8
  604.5 0.6 bitcast_dynamic-update-slice_fusion.2
  605.2 5.1 fusion.8
  610.4 0.6 bitcast_dynamic-update-slice_fusion.2
  611.0 1.7 reshape.40
  612.7 0.0 all-reduce.5.cloned.1.call-update
  612.7 45.5 %all-reduce.5.cloned.1.call-done = f32[32,2048]{1,0:T(8,128)} async-done(((f32[32,2048]{1,0:T(8,128)}), f32[32,2048]{1,0:T(8,128)}) %all-reduce.5.cloned.1.call-update) | async-done | bytes 262160 | tf_op jit(solution)/shard_map/psum | solution.py:53
  658.3 1.7 broadcast_multiply_fusion.1
  (28 shorter events, 0.2 us)
Async XLA Ops:
  6.5 1.9 copy-start
  6.5 5.1 copy-start.3
  6.5 123.6 %reduce-scatter.2.cloned.1.call-start = ((), (), s32[]{:S(2)}) async-start(), calls=%async_computation.1 | async-start | bytes 1081344 | tf_op jit(solution)/shard_map/reduce_scatter | solution.py:44
  11.5 553.0 %all-reduce.3.cloned.1.call-start = ((), (), s32[]{:S(2)}) async-start(), calls=%async_computation.2 | async-start | bytes 4194304 | tf_op jit(solution)/shard_map/psum | solution.py:51
  139.4 4.4 copy-start.2
  139.4 4.5 copy-start.4
  139.4 4.6 copy-start.1
  143.8 514.5 %all-reduce.5.cloned.1.call-start = ((), (), s32[]{:S(2)}) async-start(), calls=%async_computation.3 | async-start | bytes 524288 | tf_op jit(solution)/shard_map/psum | solution.py:53
Sparse Core Ops, SparseCore 0:
  11.7 118.4 reduce-scatter.1
  143.9 420.5 all-reduce.2
  612.9 45.3 all-reduce.4
where the time goes:
time: 667 us; the launch traced here: 666 us
  waiting for transfers between devices  585 us (88%)
  other arithmetic  47.3 us (7%)
  local copies, waits for them, and re-layouts  18.2 us (3%)
  between operations  13.2 us (2%)
    psum x1, waiting for transfers between devices, shards(): lax.psum(select_rows(base_flow, outages, first_own), ('line', 'bus'))  420 us
    reduce_scatter x1, waiting for transfers between devices, shards(): lax.psum_scatter(jnp.dot(ptdf, injections, preferred_element_type=jnp.flo...  118 us
    psum x1, waiting for transfers between devices, shards(): total = lax.psum(local_sum, 'scen')  45.5 us
    reduce_sum x8, other arithmetic, line_block(): return jnp.sum(jax.nn.sigmoid(margin), axis=2)  41.2 us
  transfers between devices with their start and end apart: 3, of which 3 were waited for; matrix products, arithmetic and copies ran while one was open for 0% of the time, Pallas kernels for 0%

commit v1 on v0

--- a/solution.py
+++ b/solution.py
@@ -48,7 +48,9 @@
         tiled=True,
     )
     first_own = (lax.axis_index("line") * lax.axis_size("bus") + lax.axis_index("bus")) * own_rows
-    outage_flow = lax.psum(select_rows(base_flow, outages, first_own), ("line", "bus"))
+    outage_flow = select_rows(base_flow, outages, first_own)
+    for axis in ("line", "bus"):
+        outage_flow = lax.psum(outage_flow, axis)
     local_sum = overload_sum(base_flow, outage_flow, lodf, ratings)
     total = lax.psum(local_sum, "scen")
     return total / (injections.shape[1] * lax.axis_size("scen"))

time: 667 us -> 625 us (0.937)
  waiting for transfers between devices: 585 us -> 542 us
    psum x1 -> x2, waiting for transfers between devices: 420 us -> 367 us  [shards(): outage_flow = lax.psum(outage_flow, axis)]
    psum x1, waiting for transfers between devices: 45.5 us -> 55.9 us  [shards(): total = lax.psum(local_sum, 'scen')]
  transfers between devices with their start and end apart: 3 -> 4, of which waited for: 3 -> 4; matrix products, arithmetic and copies ran while one was open for 0% -> 0% of each run, Pallas kernels for 0% -> 0%
where the time goes in v1:
time: 625 us; the launch traced here: 624 us
  waiting for transfers between devices  542 us (87%)
  other arithmetic  47.3 us (8%)
  local copies, waits for them, and re-layouts  18.2 us (3%)
  between operations  13.2 us (2%)
    psum x2, waiting for transfers between devices, shards(): outage_flow = lax.psum(outage_flow, axis)  367 us
    reduce_scatter x1, waiting for transfers between devices, shards(): lax.psum_scatter(jnp.dot(ptdf, injections, preferred_element_type=jnp.flo...  118 us
    psum x1, waiting for transfers between devices, shards(): total = lax.psum(local_sum, 'scen')  55.9 us
    reduce_sum x8, other arithmetic, line_block(): return jnp.sum(jax.nn.sigmoid(margin), axis=2)  41.3 us
  transfers between devices with their start and end apart: 4, of which 4 were waited for; matrix products, arithmetic and copies ran while one was open for 0% of the time, Pallas kernels for 0%

profile of v1, /device:TPU:1, one launch (start us, length us, event | category | flops | bytes accessed | tf_op | source)
XLA Modules:
  0.0 623.8 jit_solution(5935915449818516128)
XLA Ops:
  6.5 0.0 copy-start
  6.5 0.0 copy-start.3
  6.5 0.0 reduce-scatter.2.cloned.1.call-start
  6.5 1.9 copy-done
  8.4 3.1 fusion.4
  11.5 0.0 reduce-scatter.2.cloned.1.call-update
  11.5 0.0 all-reduce.4.cloned.1.call-start
  11.6 0.0 copy-done.3
  11.6 118.5 %reduce-scatter.2.cloned.1.call-done = f32[32,256]{1,0:T(8,128)} async-done(((f32[1024,256]{1,0:T(8,128)}), f32[32,256]{1,0:T(8,128)}) %reduce-scatter.2.cloned.1.call-update) | async-done | bytes 32784 | tf_op jit(solution)/shard_map/reduce_scatter | solution.py:44
  130.1 9.3 %gather_fusion = f32[2048,256]{1,0:T(8,128)} fusion(f32[32,256]{1,0:T(8,128)} %reduce-scatter.2.cloned.1.call-done, s32[2048]{0:T(1024)S(1)} %fusion.2), kind=kCustom, calls=%fused_computation | custom fusion | bytes 4202496 | tf_op jit(solution)/shard_map/jit(_take)/gather | solution.py:38
  139.4 4.3 select_select_fusion
  143.7 0.0 copy-start.2
  143.7 0.0 copy-start.4
  143.7 0.0 copy-start.1
  143.7 0.0 all-reduce.4.cloned.1.call-update
  143.8 0.0 all-reduce.6.cloned.1.call-start
  143.8 119.2 %all-reduce.4.cloned.1.call-done = f32[2048,256]{1,0:T(8,128)} async-done(((f32[2048,256]{1,0:T(8,128)}), f32[2048,256]{1,0:T(8,128)}) %all-reduce.4.cloned.1.call-update) | async-done | bytes 2097168 | tf_op jit(solution)/shard_map/psum | solution.py:53
  263.0 0.0 all-reduce.6.cloned.1.call-update
  263.1 0.0 all-reduce.8.cloned.1.call-start
  263.1 0.0 copy-done.2
  263.1 0.1 reshape.38
  263.2 0.0 copy-done.4
  263.2 0.1 reshape.39
  263.3 0.0 copy-done.1
  263.3 248.0 %all-reduce.6.cloned.1.call-done = f32[2048,256]{1,0:T(8,128)} async-done(((f32[2048,256]{1,0:T(8,128)}), f32[2048,256]{1,0:T(8,128)}) %all-reduce.6.cloned.1.call-update) | async-done | bytes 2097168 | tf_op jit(solution)/shard_map/psum | solution.py:53
  511.3 46.6 %while.10 = (s32[]{:T(128)}, f32[8,4,2048]{2,1,0:T(4,128)}, f32[8,4,256]{2,1,0:T(4,128)S(1)}, bf16[8,4,2048]{2,1,0:T(4,128)(2,1)S(1)}, f32[2048,256]{1,0:T(8,128)}, /*index=5*/f32[8,4]{1,0:T(8,128)S(1)}, s32[]{:T(128)}) while((s32[]{:T(128)}, f32[8,4,2048]{2,1,0:T(4,128)}, f32[8,4,256]{2,1,0:T(4,128)S(1)}, bf16[8,4,2048]{2,1,0:T(4,128)(2,1)S(1)}, ...), condition=%wide.region_5.6_spmd, body=%wide.region_3.5_spmd.sunk | while | flops 18874372 | bytes 2290345 | solution.py:27
  511.3 5.2 fusion.8
  516.5 0.6 bitcast_dynamic-update-slice_fusion.2
  517.1 5.2 fusion.8
  522.3 0.6 bitcast_dynamic-update-slice_fusion.2
  523.0 5.2 fusion.8
  528.1 0.6 bitcast_dynamic-update-slice_fusion.2
  528.8 5.2 fusion.8
  533.9 0.6 bitcast_dynamic-update-slice_fusion.2
  534.6 5.2 fusion.8
  539.8 0.6 bitcast_dynamic-update-slice_fusion.2
  540.4 5.2 fusion.8
  545.6 0.6 bitcast_dynamic-update-slice_fusion.2
  546.2 5.2 fusion.8
  551.4 0.6 bitcast_dynamic-update-slice_fusion.2
  552.1 5.2 fusion.8
  557.2 0.6 bitcast_dynamic-update-slice_fusion.2
  557.8 1.7 reshape.40
  559.6 0.0 all-reduce.8.cloned.1.call-update
  559.6 55.9 %all-reduce.8.cloned.1.call-done = f32[32,2048]{1,0:T(8,128)} async-done(((f32[32,2048]{1,0:T(8,128)}), f32[32,2048]{1,0:T(8,128)}) %all-reduce.8.cloned.1.call-update) | async-done | bytes 262160 | tf_op jit(solution)/shard_map/psum | solution.py:55
  615.5 1.7 broadcast_multiply_fusion.1
  (28 shorter events, 0.2 us)
Async XLA Ops:
  6.5 1.9 copy-start
  6.5 5.1 copy-start.3
  6.5 123.6 %reduce-scatter.2.cloned.1.call-start = ((), (), s32[]{:S(2)}) async-start(), calls=%async_computation.1 | async-start | bytes 1081344 | tf_op jit(solution)/shard_map/reduce_scatter | solution.py:44
  11.5 251.5 %all-reduce.4.cloned.1.call-start = ((), (), s32[]{:S(2)}) async-start(), calls=%async_computation.2 | async-start | bytes 4194304 | tf_op jit(solution)/shard_map/psum | solution.py:53
  143.7 119.4 %copy-start.2 = (bf16[32,2048]{1,0:T(8,128)(2,1)S(1)}, bf16[32,2048]{1,0:T(8,128)(2,1)}, u32[]{:S(2)}) copy-start(bf16[32,2048]{1,0:T(8,128)(2,1)} %param.9) | copy-start | bytes 393220
  143.7 119.5 %copy-start.4 = (f32[32]{0:T(128)S(1)}, f32[32]{0:T(128)}, u32[]{:S(2)}) copy-start(f32[32]{0:T(128)} %param.10) | copy-start | bytes 388
  143.7 119.5 %copy-start.1 = (f32[32,256]{1,0:T(8,128)S(1)}, f32[32,256]{1,0:T(8,128)}, u32[]{:S(2)}) copy-start(f32[32,256]{1,0:T(8,128)} %reduce-scatter.2.cloned.1.call-done) | copy-start | bytes 98308
  143.8 367.5 %all-reduce.6.cloned.1.call-start = ((), (), s32[]{:S(2)}) async-start(), calls=%async_computation.3 | async-start | bytes 4194304 | tf_op jit(solution)/shard_map/psum | solution.py:53
  263.1 352.5 %all-reduce.8.cloned.1.call-start = ((), (), s32[]{:S(2)}) async-start(), calls=%async_computation.4 | async-start | bytes 524288 | tf_op jit(solution)/shard_map/psum | solution.py:55
Sparse Core Ops, SparseCore 0:
  11.7 118.4 reduce-scatter.1
  143.9 119.1 all-reduce.3
  266.0 245.2 all-reduce.5
  559.7 55.7 all-reduce.7
